TPU v7x, 256 devices: a whole 4x4x8 slice. The times are simulated.
256 devices in a mesh: freq: 32 (over x, y, core), node: 8 (over z).
Axes of the slice: x: 4, y: 4, z: 8, core: 2. Of those that a mesh axis runs over, the one named last changes fastest.
Arguments:
- pressure: bfloat16 [2, 128, 4, 65536], P(None, 'freq', None, 'node'), may hold values from -6 to 6
- spectrum_amp: float32 [4, 128], replicated, may hold values from 0.03 to 0.3
- phase_code: int32 [4, 128], replicated, may hold values from 0 to 4095
- panel_tile: int32 [32, 8, 256, 1], P('freq'), may hold values from 0 to 255; in each aligned block of 2048 rows (0 to 2047, 2048 to 4095, ..., all dimensions but the last counted through in order) at most 12 rows name the same one
- patch_weight: bfloat16 [32, 8, 256, 128], P('freq'), may hold values from 0 to 0.099609375
Outputs:
- node_loads: bfloat16 [4, 4096, 32768], P(None, 'node', 'freq')
Inputs may be any that keep to these rules, and one draw needn't show every extreme that they name: Within each block panel_tile[g] (2048 panels), no patch is named by more than 12 panels, a bound that some block reaches; every patch is named somewhere.
All inputs are finite; a program needn't handle non-finite values.
Results may differ from a plain program's by a relative error of at most 0.0062.
Values may be sent and summed in bfloat16 or wider, within the bound.
No kernel may reach another device: no remote copies, remote signals or barrier semaphores. Data moves between devices by JAX's collectives and lax.ppermute only.
A program may use at most 128 MiB of HBM per device.

v0:
```python
import math
import jax
import jax.numpy as jnp
from jax import lax
from jax.sharding import PartitionSpec as P

F = 128
TSTEPS = 4096
BIN_STEP = 15
PHASE_LEVELS = 4096
TILE_DEV = 8


def scale_spectra(pressure, spectrum_amp, phase_code):
    phase_angle = phase_code.astype(jnp.float32) * (2.0 * math.pi / PHASE_LEVELS)
    amplitude = spectrum_amp.T[:, :, None]
    cosine = jnp.cos(phase_angle).T[:, :, None]
    sine_part = jnp.sin(phase_angle).T[:, :, None]
    real_part = pressure[0].astype(jnp.float32)
    imag_part = pressure[1].astype(jnp.float32)
    scaled_re = amplitude * (real_part * cosine - imag_part * sine_part)
    scaled_im = amplitude * (real_part * sine_part + imag_part * cosine)
    return jnp.stack([scaled_re, scaled_im]).astype(jnp.bfloat16)


def basis_table(step_count):
    freq_bin = 1 + BIN_STEP * jnp.arange(F, dtype=jnp.int32)
    step_ids = jnp.arange(step_count, dtype=jnp.int32)
    turn_count = freq_bin[:, None] * step_ids[None, :] % TSTEPS
    turn_angle = turn_count.astype(jnp.float32) * (2.0 * math.pi / TSTEPS)
    return jnp.concatenate([jnp.cos(turn_angle), -jnp.sin(turn_angle)], axis=0).astype(jnp.bfloat16)


def slot_members(tile_ids, tile_count, capacity):
    row_count = tile_ids.shape[0]
    onehot = (tile_ids[:, None] == jnp.arange(tile_count, dtype=jnp.int32)[None, :]).astype(
        jnp.int32
    )
    slot_rank = jnp.sum((jnp.cumsum(onehot, axis=0) - onehot) * onehot, axis=1)
    slot_index = tile_ids * capacity + slot_rank
    empty = jnp.full((tile_count * capacity,), row_count, jnp.int32)
    return empty.at[slot_index].set(jnp.arange(row_count, dtype=jnp.int32))


def shards(pressure, spectrum_amp, phase_code, panel_tile, patch_weight):
    regrouped = lax.all_to_all(pressure, "freq", split_axis=3, concat_axis=1, tiled=True)
    scaled = scale_spectra(regrouped, spectrum_amp, phase_code)
    freq_count = scaled.shape[1]
    headings = scaled.shape[2]
    panels = scaled.shape[3]
    owners = lax.axis_size("freq")
    windows = lax.axis_size("node")
    window_len = TSTEPS // windows
    tile_count = owners * TILE_DEV
    capacity = max(2, 3 * windows * panels // (2 * TILE_DEV * owners))
    tile_ids = panel_tile.reshape(-1)
    weights = patch_weight.reshape(-1, 128)
    members = slot_members(tile_ids, tile_count, capacity)
    sent_weight = jnp.take(weights, members, axis=0, mode="fill", fill_value=0)
    sent_weight = sent_weight.reshape(1, owners, TILE_DEV, capacity, 128)
    wave_basis = basis_table(TSTEPS)
    series = jnp.einsum(
        "khp,kt->hpt",
        scaled.reshape(2 * freq_count, headings, panels),
        wave_basis,
        preferred_element_type=jnp.float32,
    ).astype(jnp.bfloat16)
    window = lax.all_to_all(series, "node", split_axis=2, concat_axis=1, tiled=True)
    sent_rows = jnp.take(window, members, axis=1, mode="fill", fill_value=0)
    sent_rows = sent_rows.reshape(headings, owners, TILE_DEV, capacity, window_len)
    got_rows = lax.all_to_all(sent_rows, "freq", split_axis=1, concat_axis=1, tiled=True)
    got_weight = lax.all_to_all(sent_weight, "freq", split_axis=1, concat_axis=1, tiled=True)
    partial_value = jnp.einsum(
        "hskcw,skcn->hwkn", got_rows, got_weight[0], preferred_element_type=jnp.float32
    )
    node_loads = partial_value.reshape(partial_value.shape[0], partial_value.shape[1], -1)
    return node_loads.astype(jnp.bfloat16)


def solution(mesh):
    placed = (
        P(None, "freq", None, "node"),
        P(),
        P(),
        P("freq", None, None, None),
        P("freq", None, None, None),
    )
    return jax.shard_map(
        shards, mesh=mesh, in_specs=placed, out_specs=P(None, "node", "freq"), check_vma=False
    )
```

profile of v0, /device:TPU:1, one launch (start us, length us, event | category | flops | bytes accessed | tf_op | source)
XLA Modules:
  0.0 614.2 jit_solution(6448219081164938519)
XLA Ops:
  0.0 18.4 %copy.63 = bf16[2,4,4,8192]{2,1,0,3:T(4,128)(2,1)} copy(bf16[2,4,4,8192]{3,2,1,0:T(4,128)(2,1)} %param.5) | data formatting | bytes 1048576 | tf_op args[0]
  18.4 31.9 %reshape.201 = bf16[32,2,4096]{2,1,0:T(2,128)(2,1)} reshape(bf16[8192,2,4,4]{3,2,1,0:T(4,128)(2,1)} %bitcast.53) | data formatting | bytes 1048576
  50.2 8.6 %all-to-all-start.1 = ((bf16[32,2,4096]{2,1,0:T(2,128)(2,1)}), bf16[32,2,4096]{2,1,0:T(2,128)(2,1)S(1)}, u32[]{:S(2)}, u32[]{:S(2)}) async-start(bf16[32,2,4096]{2,1,0:T(2,128)(2,1)} %reshape.201), calls=%async_computation.1 | async-start | bytes 1048576 | tf_op jit(solution)/shard_map/all_to_all | solution.py:46
  59.2 9.0 %cosine_convert_fusion = (bf16[128,4096]{1,0:T(8,128)(2,1)S(1)}, bf16[128,4096]{1,0:T(8,128)(2,1)S(1)}) fusion(s32[128]{0:T(128)S(1)} %multiply_add_fusion), kind=kLoop, calls=%fused_computation.22 | loop fusion | flops 8912896 | bytes 2097664 | tf_op jit(solution)/shard_map/convert.2
  68.2 2.2 all-to-all-done.1
  70.4 37.1 %reshape.202 = bf16[8192,2,4,4]{3,2,1,0:T(4,128)(2,1)} reshape(bf16[32,2,4096]{2,1,0:T(2,128)(2,1)S(1)} %all-to-all-done.1) | data formatting | bytes 1048576
  107.6 22.6 %copy.64 = bf16[2,4,4,32,256]{4,2,1,3,0:T(4,128)(2,1)S(1)} copy(bf16[2,4,4,32,256]{2,1,0,4,3:T(4,128)(2,1)} %bitcast.52) | data formatting | bytes 1048576 | tf_op jit(solution)/shard_map/all_to_all | solution.py:46
  131.2 5.6 convolution_convert_fusion
  136.8 13.6 %copy.68 = bf16[4,256,4096]{1,0,2:T(4,128)(2,1)} copy(bf16[4,256,4096]{2,1,0:T(8,128)(2,1)} %convolution_convert_fusion) | data formatting | bytes 16777216 | tf_op jit(solution)/shard_map/convert_element_type | solution.py:67
  150.4 8.3 %all-to-all-start.2 = ((bf16[4,256,4096]{1,0,2:T(4,128)(2,1)}), bf16[4,256,4096]{1,0,2:T(4,128)(2,1)}, u32[]{:S(2)}, u32[]{:S(2)}) async-start(bf16[4,256,4096]{1,0,2:T(4,128)(2,1)} %copy.68), calls=%async_computation.2 | async-start | bytes 16777216 | tf_op jit(solution)/shard_map/all_to_all | solution.py:68
  161.7 8.1 %scatter_custom_fusion = s32[3072]{0:T(1024)S(1)} fusion(s32[2048]{0:T(1024)S(1)} %bitcast.67, s32[2048]{0:T(1024)S(1)} %iota.22, s32[]{:T(128)} %constant.33.clone.1), kind=kCustom, calls=%fused_computation.51 | custom fusion | bytes 12292 | tf_op jit(solution)/shard_map/scatter | solution.py:42
  170.0 9.2 %gather_fusion = bf16[3072,128]{1,0:T(8,128)(2,1)S(1)} fusion(bf16[2048,128]{1,0:T(8,128)(2,1)S(1)} %bitcast.51, s32[3072]{0:T(1024)S(1)} %fusion.26), kind=kCustom, calls=%fused_computation | custom fusion | bytes 1585152 | tf_op jit(solution)/shard_map/jit(_take)/gather | solution.py:59
  181.2 164.8 %all-to-all-done.2 = bf16[4,256,4096]{1,0,2:T(4,128)(2,1)} async-done(((bf16[4,256,4096]{1,0,2:T(4,128)(2,1)}), bf16[4,256,4096]{1,0,2:T(4,128)(2,1)}, u32[]{:S(2)}, u32[]{:S(2)}) %all-to-all-start.2) | async-done | bytes 8388640 | tf_op jit(solution)/shard_map/all_to_all | solution.py:68
  345.9 5.2 all-to-all-start
  351.2 7.7 %copy.69 = bf16[4,256,4096]{1,2,0:T(8,128)(2,1)} copy(bf16[4,256,4096]{1,0,2:T(4,128)(2,1)} %all-to-all-done.2) | data formatting | bytes 16777216 | tf_op jit(solution)/shard_map/all_to_all | solution.py:68
  358.9 11.4 %copy.70 = bf16[4,8,256,512]{3,2,1,0:T(8,128)(2,1)} copy(bf16[4,8,256,512]{2,3,1,0:T(8,128)(2,1)} %bitcast.55) | data formatting | bytes 16777216 | tf_op jit(solution)/shard_map/all_to_all | solution.py:68
  370.2 12.1 %copy.71 = bf16[4,2048,512]{2,0,1:T(4,128)(2,1)} copy(bf16[4,2048,512]{2,1,0:T(8,128)(2,1)} %bitcast.56) | data formatting | bytes 16777216 | tf_op jit(solution)/shard_map/all_to_all | solution.py:68
  382.4 34.7 %gather_fusion.1 = bf16[3072,4,512]{2,1,0:T(4,128)(2,1)} fusion(bf16[4,2048,512]{2,0,1:T(4,128)(2,1)} %copy.71, s32[3072]{0:T(1024)S(1)} %fusion.26), kind=kCustom, calls=%fused_computation.1 | custom fusion | bytes 25178112 | tf_op jit(solution)/shard_map/jit(_take)/gather | solution.py:69
  417.1 9.1 %broadcast_select_fusion = bf16[4,32,8,12,512]{4,0,3,2,1:T(4,128)(2,1)S(1)} fusion(bf16[4,32,8,12,512]{4,0,3,2,1:T(4,128)(2,1)} %bitcast.54, pred[32,8,12]{2,1,0:T(8,128)(4,1)S(1)} %broadcast_in_dim.35), kind=kLoop, calls=%fused_computation.5 | loop fusion | flops 6291456 | bytes 25168896 | tf_op jit(solution)/shard_map/jit(_take)/select_n | solution.py:69
  426.2 11.4 %copy.72 = bf16[4,32,8,12,512]{4,2,3,0,1:T(8,128)(2,1)} copy(bf16[4,32,8,12,512]{4,0,3,2,1:T(4,128)(2,1)S(1)} %broadcast_select_fusion) | data formatting | bytes 25165824 | tf_op jit(solution)/shard_map/jit(_take)/select_n | solution.py:69
  437.7 147.9 %all_to_all.43 = bf16[4,32,8,12,512]{4,2,3,0,1:T(8,128)(2,1)S(1)} all-to-all(bf16[4,32,8,12,512]{4,2,3,0,1:T(8,128)(2,1)} %copy.72), channel_id=1, replica_groups=mesh['freq'=32,'node'=8] {'freq'}, dimensions={1} | all-to-all | bytes 25165824 | tf_op jit(solution)/shard_map/all_to_all | solution.py:71
  585.6 17.9 %fusion.2 = bf16[4,512,8,128]{1,3,0,2:T(8,128)(2,1)} fusion(bf16[4,32,8,12,512]{4,2,3,0,1:T(8,128)(2,1)S(1)} %all_to_all.43, bf16[32,8,12,128,1]{3,1,2,0,4:T(8,128)(2,1)S(1)} %bitcast.62), kind=kOutput, calls=%fused_computation.8 | convolution fusion | flops 1612709888 | bytes 17563648 | tf_op jit(solution)/shard_map/hskcw,skcn->hwkn/dot_general | solution.py:73
  603.4 4.6 copy.74
  608.0 6.2 %copy.75 = bf16[4,512,1024]{2,1,0:T(8,128)(2,1)} copy(bf16[4,512,1024]{1,2,0:T(8,128)(2,1)} %bitcast.57) | data formatting | bytes 8388608 | tf_op jit(solution)/shard_map/convert_element_type | solution.py:77
  (36 shorter events, 6.5 us)
Async XLA Ops:
  0.0 170.0 %copy-start = (bf16[1,8,256,128]{3,2,1,0:T(8,128)(2,1)S(1)}, bf16[1,8,256,128]{3,2,1,0:T(8,128)(2,1)}, u32[]{:S(2)}) copy-start(bf16[1,8,256,128]{3,2,1,0:T(8,128)(2,1)} %param.9) | copy-start | bytes 1572868
  18.4 40.5 %copy-start.3 = (s32[4,128]{1,0:T(4,128)S(1)}, s32[4,128]{1,0:T(4,128)}, u32[]{:S(2)}) copy-start(s32[4,128]{1,0:T(4,128)} %param.7) | copy-start | bytes 6148
  18.4 40.7 %copy-start.4 = (f32[4,128]{1,0:T(4,128)S(1)}, f32[4,128]{1,0:T(4,128)}, u32[]{:S(2)}) copy-start(f32[4,128]{1,0:T(4,128)} %param.6) | copy-start | bytes 6148
  50.2 20.2 %all-to-all-start.1 = ((bf16[32,2,4096]{2,1,0:T(2,128)(2,1)}), bf16[32,2,4096]{2,1,0:T(2,128)(2,1)S(1)}, u32[]{:S(2)}, u32[]{:S(2)}) async-start(bf16[32,2,4096]{2,1,0:T(2,128)(2,1)} %reshape.201), calls=%async_computation.1 | async-start | bytes 1048576 | tf_op jit(solution)/shard_map/all_to_all | solution.py:46
  150.4 8.3 %copy-start.2 = (s32[1,8,256,1]{2,3,1,0:T(1,128)S(1)}, s32[1,8,256,1]{2,3,1,0:T(1,128)}, u32[]{:S(2)}) copy-start(s32[1,8,256,1]{2,3,1,0:T(1,128)} %param.8) | copy-start | bytes 24580
  150.4 195.5 %all-to-all-start.2 = ((bf16[4,256,4096]{1,0,2:T(4,128)(2,1)}), bf16[4,256,4096]{1,0,2:T(4,128)(2,1)}, u32[]{:S(2)}, u32[]{:S(2)}) async-start(bf16[4,256,4096]{1,0,2:T(4,128)(2,1)} %copy.68), calls=%async_computation.2 | async-start | bytes 16777216 | tf_op jit(solution)/shard_map/all_to_all | solution.py:68
  345.9 91.7 %all-to-all-start = ((bf16[1,32,8,12,128]{4,2,3,0,1:T(8,128)(2,1)}), bf16[1,32,8,12,128]{4,2,3,0,1:T(8,128)(2,1)S(1)}, u32[]{:S(2)}, u32[]{:S(2)}) async-start(bf16[1,32,8,12,128]{4,2,3,0,1:T(8,128)(2,1)} %copy.60), calls=%async_computation | async-start | bytes 1572864 | tf_op jit(solution)/shard_map/all_to_all | solution.py:72
  608.0 6.3 %copy-start.1 = (bf16[1,8,256,128]{3,2,1,0:T(8,128)(2,1)S(1)}, bf16[1,8,256,128]{3,2,1,0:T(8,128)(2,1)}, u32[]{:S(2)}) copy-start(bf16[1,8,256,128]{3,2,1,0:T(8,128)(2,1)} %param.9) | copy-start | bytes 1572868
where the time goes:
time: 618 us; the launch traced here: 614 us
  local copies, waits for them, and re-layouts  232 us (38%)
  waiting for transfers between devices  167 us (27%)
  blocking collectives  148 us (24%)
  matrix products  23.5 us (4%)
  starting transfers between devices  22.1 us (4%)
  other arithmetic  21.3 us (3%)
    all_to_all x1, waiting for transfers between devices, shards(): lax.all_to_all(series, 'node', split_axis=2, concat_axis=1, tiled=True)  165 us
    all_to_all x1, blocking collectives, shards(): lax.all_to_all(sent_rows, 'freq', split_axis=1, concat_axis=1, tiled=True)  148 us
    unnamed x13, local copies, waits for them, and re-layouts  87.4 us
    gather x1, local copies, waits for them, and re-layouts, shards(): sent_rows = jnp.take(window, members, axis=1, mode='fill', fill_value=0)  34.7 us
    all_to_all x3, local copies, waits for them, and re-layouts, shards(): lax.all_to_all(series, 'node', split_axis=2, concat_axis=1, tiled=True)  31.2 us
    all_to_all x1, local copies, waits for them, and re-layouts, shards(): lax.all_to_all(pressure, 'freq', split_axis=3, concat_axis=1, tiled=True)  22.6 us
    dot_general x1, matrix products, shards(): jnp.einsum('hskcw,skcn->hwkn', got_rows, got_weight[0], preferred_element...  17.9 us
    convert_element_type x1, local copies, waits for them, and re-layouts, shards(): series = jnp.einsum('khp,kt->hpt', scaled.reshape(2 * freq_count, heading...  13.6 us
  transfers between devices with their start and end apart: 3, of which 2 were waited for; matrix products, arithmetic and copies ran while one was open for 19% of the time, Pallas kernels for 0%

commit v1 on v0

--- a/solution.py
+++ b/solution.py
@@ -43,7 +43,10 @@
 
 
 def shards(pressure, spectrum_amp, phase_code, panel_tile, patch_weight):
-    regrouped = lax.all_to_all(pressure, "freq", split_axis=3, concat_axis=1, tiled=True)
+    regrouped = jnp.concatenate(
+        lax.all_to_all(jnp.stack(jnp.split(pressure, lax.axis_size("freq"), axis=3)), "freq", 0, 0),
+        axis=1,
+    )
     scaled = scale_spectra(regrouped, spectrum_amp, phase_code)
     freq_count = scaled.shape[1]
     headings = scaled.shape[2]

time: 618 us -> 549 us (0.89)
  local copies, waits for them, and re-layouts: 232 us -> 165 us
    unnamed x13 -> x41, local copies, waits for them, and re-layouts: 87.4 us -> 41.3 us
    all_to_all x1 -> x0, local copies, waits for them, and re-layouts: 22.6 us -> none  [shards(): lax.all_to_all(pressure, 'freq', split_axis=3, concat_axis=1, tiled=True)]
  transfers between devices with their start and end apart: 3 -> 3, of which waited for: 2 -> 2; matrix products, arithmetic and copies ran while one was open for 19% -> 22% of each run, Pallas kernels for 0% -> 0%
where the time goes in v1:
time: 549 us; the launch traced here: 546 us
  waiting for transfers between devices  167 us (30%)
  local copies, waits for them, and re-layouts  165 us (30%)
  blocking collectives  148 us (27%)
  matrix products  23.5 us (4%)
  starting transfers between devices  21.8 us (4%)
  other arithmetic  20.9 us (4%)
    all_to_all x1, waiting for transfers between devices, shards(): lax.all_to_all(series, 'node', split_axis=2, concat_axis=1, tiled=True)  165 us
    all_to_all x1, blocking collectives, shards(): lax.all_to_all(sent_rows, 'freq', split_axis=1, concat_axis=1, tiled=True)  148 us
    unnamed x41, local copies, waits for them, and re-layouts  41.3 us
    gather x1, local copies, waits for them, and re-layouts, shards(): sent_rows = jnp.take(window, members, axis=1, mode='fill', fill_value=0)  34.7 us
    all_to_all x3, local copies, waits for them, and re-layouts, shards(): lax.all_to_all(series, 'node', split_axis=2, concat_axis=1, tiled=True)  31.2 us
    dot_general x1, matrix products, shards(): jnp.einsum('hskcw,skcn->hwkn', got_rows, got_weight[0], preferred_element...  17.9 us
    convert_element_type x1, local copies, waits for them, and re-layouts, shards(): series = jnp.einsum('khp,kt->hpt', scaled.reshape(2 * freq_count, heading...  13.6 us
    select_n x1, local copies, waits for them, and re-layouts, shards(): sent_rows = jnp.take(window, members, axis=1, mode='fill', fill_value=0)  11.4 us
  transfers between devices with their start and end apart: 3, of which 2 were waited for; matrix products, arithmetic and copies ran while one was open for 22% of the time, Pallas kernels for 0%

profile of v1, /device:TPU:1, one launch (start us, length us, event | category | flops | bytes accessed | tf_op | source)
XLA Modules:
  0.0 546.2 jit_solution(18132354330567505870)
XLA Ops:
  0.0 1.4 constant_dynamic-update-slice_fusion.31
  1.4 1.3 constant_dynamic-update-slice_fusion.30
  2.7 1.3 constant_dynamic-update-slice_fusion.29
  18.7 1.3 constant_dynamic-update-slice_fusion.17
  42.6 8.6 %all-to-all-start.1 = ((bf16[32,2,4,4,256]{4,3,2,1,0:T(4,128)(2,1)}), bf16[32,2,4,4,256]{4,3,2,1,0:T(4,128)(2,1)S(1)}, u32[]{:S(2)}, u32[]{:S(2)}) async-start(bf16[32,2,4,4,256]{4,3,2,1,0:T(4,128)(2,1)} %constant_dynamic-update-slice_fusion), calls=%async_computation.1 | async-start | bytes 1048576 | tf_op jit(solution)/shard_map/all_to_all | solution.py:47
  51.2 9.0 %cosine_convert_fusion = (bf16[128,4096]{1,0:T(8,128)(2,1)S(1)}, bf16[128,4096]{1,0:T(8,128)(2,1)S(1)}) fusion(s32[128]{0:T(128)S(1)} %multiply_add_fusion), kind=kLoop, calls=%fused_computation.22 | loop fusion | flops 8912896 | bytes 2097664 | tf_op jit(solution)/shard_map/convert.2
  60.3 2.5 all-to-all-done.1
  63.5 5.6 %convolution_convert_fusion = bf16[4,256,4096]{2,1,0:T(8,128)(2,1)} fusion(bf16[256,4,256]{2,0,1:T(8,128)(2,1)S(1)} %bitcast.119, bf16[128,4096]{1,0:T(8,128)(2,1)S(1)} %get-tuple-element.12, bf16[128,4096]{1,0:T(8,128)(2,1)S(1)} %get-tuple-element.11), kind=kOutput, calls=%fused_computation.7 | convolution fusion | flops 2155872256 | bytes 11010048 | tf_op jit(solution)/shard_map/khp,kt->hpt/dot_general | solution.py:65
  69.1 13.6 %copy.93 = bf16[4,256,4096]{1,0,2:T(4,128)(2,1)} copy(bf16[4,256,4096]{2,1,0:T(8,128)(2,1)} %convolution_convert_fusion) | data formatting | bytes 16777216 | tf_op jit(solution)/shard_map/convert_element_type | solution.py:70
  82.7 8.3 %all-to-all-start.2 = ((bf16[4,256,4096]{1,0,2:T(4,128)(2,1)}), bf16[4,256,4096]{1,0,2:T(4,128)(2,1)}, u32[]{:S(2)}, u32[]{:S(2)}) async-start(bf16[4,256,4096]{1,0,2:T(4,128)(2,1)} %copy.93), calls=%async_computation.2 | async-start | bytes 16777216 | tf_op jit(solution)/shard_map/all_to_all | solution.py:71
  94.0 8.1 %scatter_custom_fusion = s32[3072]{0:T(1024)S(1)} fusion(s32[2048]{0:T(1024)S(1)} %bitcast.127, s32[2048]{0:T(1024)S(1)} %iota.22, s32[]{:T(128)} %constant.33.clone.1), kind=kCustom, calls=%fused_computation.74 | custom fusion | bytes 12292 | tf_op jit(solution)/shard_map/scatter | solution.py:42
  102.3 9.2 %gather_fusion = bf16[3072,128]{1,0:T(8,128)(2,1)S(1)} fusion(bf16[2048,128]{1,0:T(8,128)(2,1)S(1)} %bitcast.113, s32[3072]{0:T(1024)S(1)} %fusion.19), kind=kCustom, calls=%fused_computation | custom fusion | bytes 1585152 | tf_op jit(solution)/shard_map/jit(_take)/gather | solution.py:62
  113.5 164.8 %all-to-all-done.2 = bf16[4,256,4096]{1,0,2:T(4,128)(2,1)} async-done(((bf16[4,256,4096]{1,0,2:T(4,128)(2,1)}), bf16[4,256,4096]{1,0,2:T(4,128)(2,1)}, u32[]{:S(2)}, u32[]{:S(2)}) %all-to-all-start.2) | async-done | bytes 8388640 | tf_op jit(solution)/shard_map/all_to_all | solution.py:71
  278.2 4.9 all-to-all-start
  283.1 7.7 %copy.94 = bf16[4,256,4096]{1,2,0:T(8,128)(2,1)} copy(bf16[4,256,4096]{1,0,2:T(4,128)(2,1)} %all-to-all-done.2) | data formatting | bytes 16777216 | tf_op jit(solution)/shard_map/all_to_all | solution.py:71
  290.8 11.4 %copy.95 = bf16[4,8,256,512]{3,2,1,0:T(8,128)(2,1)} copy(bf16[4,8,256,512]{2,3,1,0:T(8,128)(2,1)} %bitcast.115) | data formatting | bytes 16777216 | tf_op jit(solution)/shard_map/all_to_all | solution.py:71
  302.2 12.1 %copy.96 = bf16[4,2048,512]{2,0,1:T(4,128)(2,1)} copy(bf16[4,2048,512]{2,1,0:T(8,128)(2,1)} %bitcast.116) | data formatting | bytes 16777216 | tf_op jit(solution)/shard_map/all_to_all | solution.py:71
  314.3 34.7 %gather_fusion.1 = bf16[3072,4,512]{2,1,0:T(4,128)(2,1)} fusion(bf16[4,2048,512]{2,0,1:T(4,128)(2,1)} %copy.96, s32[3072]{0:T(1024)S(1)} %fusion.19), kind=kCustom, calls=%fused_computation.1 | custom fusion | bytes 25178112 | tf_op jit(solution)/shard_map/jit(_take)/gather | solution.py:72
  349.1 9.1 %broadcast_select_fusion = bf16[4,32,8,12,512]{4,0,3,2,1:T(4,128)(2,1)S(1)} fusion(bf16[4,32,8,12,512]{4,0,3,2,1:T(4,128)(2,1)} %bitcast.114, pred[32,8,12]{2,1,0:T(8,128)(4,1)S(1)} %broadcast_in_dim.35), kind=kLoop, calls=%fused_computation.5 | loop fusion | flops 6291456 | bytes 25168896 | tf_op jit(solution)/shard_map/jit(_take)/select_n | solution.py:72
  358.2 11.4 %copy.97 = bf16[4,32,8,12,512]{4,2,3,0,1:T(8,128)(2,1)} copy(bf16[4,32,8,12,512]{4,0,3,2,1:T(4,128)(2,1)S(1)} %broadcast_select_fusion) | data formatting | bytes 25165824 | tf_op jit(solution)/shard_map/jit(_take)/select_n | solution.py:72
  369.6 147.9 %all_to_all.33 = bf16[4,32,8,12,512]{4,2,3,0,1:T(8,128)(2,1)S(1)} all-to-all(bf16[4,32,8,12,512]{4,2,3,0,1:T(8,128)(2,1)} %copy.97), channel_id=1, replica_groups=mesh['freq'=32,'node'=8] {'freq'}, dimensions={1} | all-to-all | bytes 25165824 | tf_op jit(solution)/shard_map/all_to_all | solution.py:74
  517.5 17.9 %fusion.2 = bf16[4,512,8,128]{1,3,0,2:T(8,128)(2,1)} fusion(bf16[4,32,8,12,512]{4,2,3,0,1:T(8,128)(2,1)S(1)} %all_to_all.33, bf16[32,8,12,128,1]{3,1,2,0,4:T(8,128)(2,1)S(1)} %bitcast.122), kind=kOutput, calls=%fused_computation.8 | convolution fusion | flops 1612709888 | bytes 17563648 | tf_op jit(solution)/shard_map/hskcw,skcn->hwkn/dot_general | solution.py:76
  535.4 4.6 copy.99
  539.9 6.2 %copy.100 = bf16[4,512,1024]{2,1,0:T(8,128)(2,1)} copy(bf16[4,512,1024]{1,2,0:T(8,128)(2,1)} %bitcast.117) | data formatting | bytes 8388608 | tf_op jit(solution)/shard_map/convert_element_type | solution.py:80
  (64 shorter events, 43.0 us)
Async XLA Ops:
  0.0 102.3 %copy-start = (bf16[1,8,256,128]{3,2,1,0:T(8,128)(2,1)S(1)}, bf16[1,8,256,128]{3,2,1,0:T(8,128)(2,1)}, u32[]{:S(2)}) copy-start(bf16[1,8,256,128]{3,2,1,0:T(8,128)(2,1)} %param.9) | copy-start | bytes 1572868
  0.0 60.2 %copy-start.4 = (s32[4,128]{1,0:T(4,128)S(1)}, s32[4,128]{1,0:T(4,128)}, u32[]{:S(2)}) copy-start(s32[4,128]{1,0:T(4,128)} %param.7) | copy-start | bytes 6148
  42.6 20.2 %all-to-all-start.1 = ((bf16[32,2,4,4,256]{4,3,2,1,0:T(4,128)(2,1)}), bf16[32,2,4,4,256]{4,3,2,1,0:T(4,128)(2,1)S(1)}, u32[]{:S(2)}, u32[]{:S(2)}) async-start(bf16[32,2,4,4,256]{4,3,2,1,0:T(4,128)(2,1)} %constant_dynamic-update-slice_fusion), calls=%async_computation.1 | async-start | bytes 1048576 | tf_op jit(solution)/shard_map/all_to_all | solution.py:47
  51.2 11.9 %copy-start.3 = (f32[4,128]{1,0:T(4,128)S(1)}, f32[4,128]{1,0:T(4,128)}, u32[]{:S(2)}) copy-start(f32[4,128]{1,0:T(4,128)} %param.6) | copy-start | bytes 6148
  82.7 8.3 %copy-start.2 = (s32[1,8,256,1]{2,3,1,0:T(1,128)S(1)}, s32[1,8,256,1]{2,3,1,0:T(1,128)}, u32[]{:S(2)}) copy-start(s32[1,8,256,1]{2,3,1,0:T(1,128)} %param.8) | copy-start | bytes 24580
  82.7 195.5 %all-to-all-start.2 = ((bf16[4,256,4096]{1,0,2:T(4,128)(2,1)}), bf16[4,256,4096]{1,0,2:T(4,128)(2,1)}, u32[]{:S(2)}, u32[]{:S(2)}) async-start(bf16[4,256,4096]{1,0,2:T(4,128)(2,1)} %copy.93), calls=%async_computation.2 | async-start | bytes 16777216 | tf_op jit(solution)/shard_map/all_to_all | solution.py:71
  278.2 91.4 %all-to-all-start = ((bf16[1,32,8,12,128]{4,2,3,0,1:T(8,128)(2,1)}), bf16[1,32,8,12,128]{4,2,3,0,1:T(8,128)(2,1)S(1)}, u32[]{:S(2)}, u32[]{:S(2)}) async-start(bf16[1,32,8,12,128]{4,2,3,0,1:T(8,128)(2,1)} %copy.87), calls=%async_computation | async-start | bytes 1572864 | tf_op jit(solution)/shard_map/all_to_all | solution.py:75
  539.9 6.3 %copy-start.1 = (bf16[1,8,256,128]{3,2,1,0:T(8,128)(2,1)S(1)}, bf16[1,8,256,128]{3,2,1,0:T(8,128)(2,1)}, u32[]{:S(2)}) copy-start(bf16[1,8,256,128]{3,2,1,0:T(8,128)(2,1)} %param.9) | copy-start | bytes 1572868
